TPU v7x, 128 devices: a whole 4x4x4 slice. The times are simulated.
128 devices in a mesh: tm: 8 (over x, core), dom: 16 (over z, y).
Axes of the slice: x: 4, y: 4, z: 4, core: 2. Of those that a mesh axis runs over, the one named last changes fastest.
Arguments:
- features: bfloat16 [16, 8192, 128], P('tm', 'dom'), may hold values from -6 to 6
- tile_values: bfloat16 [16, 64, 16, 4, 128, 128], P('tm', 'dom'), may hold values from -0.09375 to 0.09375
- tile_cols: int32 [16, 64, 16, 4], P('tm', 'dom'), may hold values from 0 to 3
- tile_count: int32 [16, 64, 16], P('tm', 'dom'), may hold values from 0 to 4, as said below
- hidden_start: float32 [8192, 512], P('dom'), may hold values from -4 to 4
- w_graph: bfloat16 [128, 512], replicated, may hold values from -0.5 to 0.5
- w_input: bfloat16 [512, 1536], replicated, may hold values from -0.25 to 0.25
- w_hidden: bfloat16 [512, 1536], replicated, may hold values from -0.25 to 0.25
- update_bias: float32 [512], replicated, may hold values from -1 to 4
Outputs:
- hidden_seq: bfloat16 [16, 8192, 512], P('tm', 'dom')
Inputs may be any that keep to these rules, and one draw needn't show every extreme that they name: `tile_count`: number of live slots; for each row block the entry of its own partition is 4.
All inputs are finite; a program needn't handle non-finite values.
Results may differ from a plain program's by a relative error of at most 0.0052.
Values may be sent and summed in bfloat16 or wider, within the bound.
A program may use at most 128 MiB of HBM per device.

v0:
```python
import jax
import jax.numpy as jnp
from jax import lax
from jax.sharding import PartitionSpec as P


def shifted(block, axis, distance):
    devices = range(lax.axis_size(axis))
    route = [((i - distance) % len(devices), i) for i in devices]
    return lax.ppermute(block, axis, route)


def gru_cell(state, gx, w_hidden, update_bias, hid):
    gh = jnp.dot(state.astype(jnp.bfloat16), w_hidden, preferred_element_type=jnp.float32)
    reset = jax.nn.sigmoid(gx[:, :hid] + gh[:, :hid])
    update = jax.nn.sigmoid(gx[:, hid : 2 * hid] + gh[:, hid : 2 * hid] + update_bias)
    cand = jnp.tanh(gx[:, 2 * hid :] + reset * gh[:, 2 * hid :])
    return update * state + (1.0 - update) * cand


def per_device(
    features,
    tile_values,
    tile_cols,
    tile_count,
    hidden_start,
    w_graph,
    w_input,
    w_hidden,
    update_bias,
):
    snaps, nodes, feats = features.shape
    hid = w_graph.shape[1]
    blk = tile_values.shape[-1]
    slot_count = tile_cols.shape[-1]
    nblocks = nodes // blk
    parts = lax.axis_size("dom")
    me_dom = lax.axis_index("dom")
    projected = jnp.einsum(
        "snf,fh->snh", features, w_graph, preferred_element_type=jnp.float32
    ).astype(jnp.bfloat16)
    live = jnp.arange(slot_count, dtype=jnp.int32)[None, None, None, :] < tile_count[..., None]
    masked = tile_values * live[..., None, None].astype(jnp.bfloat16)

    def partner_sum(rows, source):
        tiles_src = lax.dynamic_index_in_dim(masked, source, axis=2, keepdims=False)
        cols_src = lax.dynamic_index_in_dim(tile_cols, source, axis=2, keepdims=False)
        blocks = rows.reshape(snaps, nblocks, blk, hid)
        picked = jax.vmap(lambda block_set, col_set: block_set[col_set])(blocks, cols_src)
        return jnp.einsum(
            "snkij,snkjh->snih", tiles_src, picked, preferred_element_type=jnp.float32
        )

    total = partner_sum(projected, me_dom)

    def loop_step(step, carry):
        rows, acc = carry
        rows = shifted(rows, "dom", 1)
        source = (me_dom - step) % parts
        return (rows, acc + partner_sum(rows, source))

    moved, total = lax.fori_loop(1, parts, loop_step, (projected, total))
    propagated = total.reshape(snaps, nodes, hid)
    graph_out = jax.nn.relu(propagated).astype(jnp.bfloat16)
    sections = lax.axis_size("tm")
    me_time = lax.axis_index("tm")
    mine = lax.all_to_all(graph_out, "tm", split_axis=1, concat_axis=0, tiled=True)
    share = nodes // sections
    start_rows = lax.dynamic_slice_in_dim(hidden_start, me_time * share, share, 0)

    def scan_cell(state, graph_row):
        gx = jnp.dot(graph_row, w_input, preferred_element_type=jnp.float32)
        state = gru_cell(state, gx, w_hidden, update_bias, hid)
        return (state, state.astype(jnp.bfloat16))

    last_state, own_seq = lax.scan(scan_cell, start_rows, mine)
    hidden_seq = lax.all_to_all(own_seq, "tm", split_axis=0, concat_axis=1, tiled=True)
    return hidden_seq


def solution(mesh):
    placed = (
        P("tm", "dom", None),
        P("tm", "dom", None, None, None, None),
        P("tm", "dom", None, None),
        P("tm", "dom", None),
        P("dom", None),
        P(),
        P(),
        P(),
        P(),
    )
    return jax.shard_map(
        per_device, mesh=mesh, in_specs=placed, out_specs=P("tm", "dom", None), check_vma=False
    )
```

profile of v0, /device:TPU:1, one launch (start us, length us, event | category | flops | bytes accessed | tf_op | source)
XLA Modules:
  0.0 593.3 jit_solution(4819321105455400747)
XLA Ops:
  7.1 8.5 %copy_multiply_fusion = bf16[2,4,16,4,128,128]{5,4,3,1,0,2:T(8,128)(2,1)S(1)} fusion(bf16[2,4,16,4,128,128]{5,4,3,2,1,0:T(8,128)(2,1)} %param.14, bf16[2,4,16,4]{3,1,0,2:T(4,128)(2,1)S(1)} %fusion.28), kind=kLoop, calls=%fused_computation.33 | loop fusion | flops 8388608 | bytes 33555456 | tf_op jit(solution)/shard_map/mul | solution.py:43
  22.0 450.5 %while.29 = (s32[]{:T(128)}, bf16[2,512,512]{2,1,0:T(8,128)(2,1)S(1)}, f32[2,4,128,512]{3,2,1,0:T(8,128)}, s32[]{:T(128)}, bf16[2,4,16,4,128,128]{5,4,3,1,0,2:T(...) while((s32[]{:T(128)}, ...), condition=%wide.region_1.2_spmd, body=%wide.region_0.1_spmd.sunk | while | flops 537395456 | bytes 24118320 | solution.py:62
  24.2 27.7 %collective-permute-done = bf16[2,512,512]{2,1,0:T(8,128)(2,1)S(1)} collective-permute-done((bf16[2,512,512]{2,1,0:T(8,128)(2,1)S(1)}, bf16[2,512,512]{2,1,0:T(8,128)(2,1)S(1)}, u32[]{:S(2)}, u32[]{:S(2)}) %collective-permute-start) | collective-permute-done | bytes 1048608 | tf_op jit(solution)/shard_map/while/body/eval_jaxpr/ppermute | solution.py:10
  54.6 5.2 bitcast_add_fusion.2
  60.1 26.6 %collective-permute-done = bf16[2,512,512]{2,1,0:T(8,128)(2,1)S(1)} collective-permute-done((bf16[2,512,512]{2,1,0:T(8,128)(2,1)S(1)}, bf16[2,512,512]{2,1,0:T(8,128)(2,1)S(1)}, u32[]{:S(2)}, u32[]{:S(2)}) %collective-permute-start) | collective-permute-done | bytes 1048608 | tf_op jit(solution)/shard_map/while/body/eval_jaxpr/ppermute | solution.py:10
  95.0 25.8 %collective-permute-done = bf16[2,512,512]{2,1,0:T(8,128)(2,1)S(1)} collective-permute-done((bf16[2,512,512]{2,1,0:T(8,128)(2,1)S(1)}, bf16[2,512,512]{2,1,0:T(8,128)(2,1)S(1)}, u32[]{:S(2)}, u32[]{:S(2)}) %collective-permute-start) | collective-permute-done | bytes 1048608 | tf_op jit(solution)/shard_map/while/body/eval_jaxpr/ppermute | solution.py:10
  123.5 5.2 bitcast_add_fusion.2
  129.1 24.9 %collective-permute-done = bf16[2,512,512]{2,1,0:T(8,128)(2,1)S(1)} collective-permute-done((bf16[2,512,512]{2,1,0:T(8,128)(2,1)S(1)}, bf16[2,512,512]{2,1,0:T(8,128)(2,1)S(1)}, u32[]{:S(2)}, u32[]{:S(2)}) %collective-permute-start) | collective-permute-done | bytes 1048608 | tf_op jit(solution)/shard_map/while/body/eval_jaxpr/ppermute | solution.py:10
  156.7 5.2 bitcast_add_fusion.2
  162.2 24.1 %collective-permute-done = bf16[2,512,512]{2,1,0:T(8,128)(2,1)S(1)} collective-permute-done((bf16[2,512,512]{2,1,0:T(8,128)(2,1)S(1)}, bf16[2,512,512]{2,1,0:T(8,128)(2,1)S(1)}, u32[]{:S(2)}, u32[]{:S(2)}) %collective-permute-start) | collective-permute-done | bytes 1048608 | tf_op jit(solution)/shard_map/while/body/eval_jaxpr/ppermute | solution.py:10
  189.1 5.2 bitcast_add_fusion.2
  194.6 23.2 %collective-permute-done = bf16[2,512,512]{2,1,0:T(8,128)(2,1)S(1)} collective-permute-done((bf16[2,512,512]{2,1,0:T(8,128)(2,1)S(1)}, bf16[2,512,512]{2,1,0:T(8,128)(2,1)S(1)}, u32[]{:S(2)}, u32[]{:S(2)}) %collective-permute-start) | collective-permute-done | bytes 1048608 | tf_op jit(solution)/shard_map/while/body/eval_jaxpr/ppermute | solution.py:10
  220.5 5.2 bitcast_add_fusion.2
  226.1 22.4 %collective-permute-done = bf16[2,512,512]{2,1,0:T(8,128)(2,1)S(1)} collective-permute-done((bf16[2,512,512]{2,1,0:T(8,128)(2,1)S(1)}, bf16[2,512,512]{2,1,0:T(8,128)(2,1)S(1)}, u32[]{:S(2)}, u32[]{:S(2)}) %collective-permute-start) | collective-permute-done | bytes 1048608 | tf_op jit(solution)/shard_map/while/body/eval_jaxpr/ppermute | solution.py:10
  251.2 5.2 bitcast_add_fusion.2
  256.7 21.5 %collective-permute-done = bf16[2,512,512]{2,1,0:T(8,128)(2,1)S(1)} collective-permute-done((bf16[2,512,512]{2,1,0:T(8,128)(2,1)S(1)}, bf16[2,512,512]{2,1,0:T(8,128)(2,1)S(1)}, u32[]{:S(2)}, u32[]{:S(2)}) %collective-permute-start) | collective-permute-done | bytes 1048608 | tf_op jit(solution)/shard_map/while/body/eval_jaxpr/ppermute | solution.py:10
  286.4 20.6 %collective-permute-done = bf16[2,512,512]{2,1,0:T(8,128)(2,1)S(1)} collective-permute-done((bf16[2,512,512]{2,1,0:T(8,128)(2,1)S(1)}, bf16[2,512,512]{2,1,0:T(8,128)(2,1)S(1)}, u32[]{:S(2)}, u32[]{:S(2)}) %collective-permute-start) | collective-permute-done | bytes 1048608 | tf_op jit(solution)/shard_map/while/body/eval_jaxpr/ppermute | solution.py:10
  309.8 5.2 bitcast_add_fusion.2
  315.4 19.8 %collective-permute-done = bf16[2,512,512]{2,1,0:T(8,128)(2,1)S(1)} collective-permute-done((bf16[2,512,512]{2,1,0:T(8,128)(2,1)S(1)}, bf16[2,512,512]{2,1,0:T(8,128)(2,1)S(1)}, u32[]{:S(2)}, u32[]{:S(2)}) %collective-permute-start) | collective-permute-done | bytes 1048608 | tf_op jit(solution)/shard_map/while/body/eval_jaxpr/ppermute | solution.py:10
  337.9 5.2 bitcast_add_fusion.2
  343.4 18.9 %collective-permute-done = bf16[2,512,512]{2,1,0:T(8,128)(2,1)S(1)} collective-permute-done((bf16[2,512,512]{2,1,0:T(8,128)(2,1)S(1)}, bf16[2,512,512]{2,1,0:T(8,128)(2,1)S(1)}, u32[]{:S(2)}, u32[]{:S(2)}) %collective-permute-start) | collective-permute-done | bytes 1048608 | tf_op jit(solution)/shard_map/while/body/eval_jaxpr/ppermute | solution.py:10
  365.1 5.2 bitcast_add_fusion.2
  370.6 18.1 %collective-permute-done = bf16[2,512,512]{2,1,0:T(8,128)(2,1)S(1)} collective-permute-done((bf16[2,512,512]{2,1,0:T(8,128)(2,1)S(1)}, bf16[2,512,512]{2,1,0:T(8,128)(2,1)S(1)}, u32[]{:S(2)}, u32[]{:S(2)}) %collective-permute-start) | collective-permute-done | bytes 1048608 | tf_op jit(solution)/shard_map/while/body/eval_jaxpr/ppermute | solution.py:10
  397.0 17.2 %collective-permute-done = bf16[2,512,512]{2,1,0:T(8,128)(2,1)S(1)} collective-permute-done((bf16[2,512,512]{2,1,0:T(8,128)(2,1)S(1)}, bf16[2,512,512]{2,1,0:T(8,128)(2,1)S(1)}, u32[]{:S(2)}, u32[]{:S(2)}) %collective-permute-start) | collective-permute-done | bytes 1048608 | tf_op jit(solution)/shard_map/while/body/eval_jaxpr/ppermute | solution.py:10
  422.4 16.8 %collective-permute-done = bf16[2,512,512]{2,1,0:T(8,128)(2,1)S(1)} collective-permute-done((bf16[2,512,512]{2,1,0:T(8,128)(2,1)S(1)}, bf16[2,512,512]{2,1,0:T(8,128)(2,1)S(1)}, u32[]{:S(2)}, u32[]{:S(2)}) %collective-permute-start) | collective-permute-done | bytes 1048608 | tf_op jit(solution)/shard_map/while/body/eval_jaxpr/ppermute | solution.py:10
  442.0 5.2 bitcast_add_fusion.2
  447.5 16.8 %collective-permute-done = bf16[2,512,512]{2,1,0:T(8,128)(2,1)S(1)} collective-permute-done((bf16[2,512,512]{2,1,0:T(8,128)(2,1)S(1)}, bf16[2,512,512]{2,1,0:T(8,128)(2,1)S(1)}, u32[]{:S(2)}, u32[]{:S(2)}) %collective-permute-start) | collective-permute-done | bytes 1048608 | tf_op jit(solution)/shard_map/while/body/eval_jaxpr/ppermute | solution.py:10
  467.1 5.2 bitcast_add_fusion.2
  476.4 18.2 %all-to-all-start = ((bf16[2,512,512]{2,0,1:T(2,128)(2,1)}), bf16[2,512,512]{2,0,1:T(2,128)(2,1)}, u32[]{:S(2)}, u32[]{:S(2)}) async-start(bf16[2,512,512]{2,0,1:T(2,128)(2,1)} %bitcast.70), calls=%async_computation | async-start | bytes 2097152 | tf_op jit(solution)/shard_map/all_to_all | solution.py:67
  494.6 15.1 %all-to-all-done = bf16[2,512,512]{2,0,1:T(2,128)(2,1)} async-done(((bf16[2,512,512]{2,0,1:T(2,128)(2,1)}), bf16[2,512,512]{2,0,1:T(2,128)(2,1)}, u32[]{:S(2)}, u32[]{:S(2)}) %all-to-all-start) | async-done | bytes 1048608 | tf_op jit(solution)/shard_map/all_to_all | solution.py:67
  512.2 60.7 %while.30 = (s32[]{:T(128)}, f32[64,512]{1,0:T(8,128)S(1)}, bf16[16,64,512]{2,1,0:T(8,128)(2,1)}, bf16[16,64,512]{2,1,0:T(8,128)(2,1)}, bf16[512,1536]{1,0:T(8,1...) while((s32[]{:T(128)}, f32[64,512]{1,0:T(8,128)S(1)}, ...), condition=%wide.region_3.4_spmd, body=%wide.region_2.3_spmd.sunk | while | flops 201883648 | bytes 5246037 | solution.py:76
  572.8 19.4 %all_to_all.36 = bf16[16,64,512]{2,1,0:T(8,128)(2,1)S(1)} all-to-all(bf16[16,64,512]{2,1,0:T(8,128)(2,1)} %get-tuple-element.198), channel_id=1, replica_groups=mesh['tm'=8,'dom'=16] {'tm'}, dimensions={0} | all-to-all | bytes 2097152 | tf_op jit(solution)/shard_map/all_to_all | solution.py:77
  (153 shorter events, 149.2 us)
Async XLA Ops:
  0.0 494.6 %copy-start = (f32[512,512]{1,0:T(8,128)S(1)}, f32[512,512]{1,0:T(8,128)}, u32[]{:S(2)}) copy-start(f32[512,512]{1,0:T(8,128)} %param.17) | copy-start | bytes 3145732
  7.1 8.5 %copy-start.3 = (bf16[32,128,512]{2,1,0:T(8,128)(2,1)S(1)}, bf16[32,128,512]{2,1,0:T(8,128)(2,1)}, u32[]{:S(2)}) copy-start(bf16[32,128,512]{2,1,0:T(8,128)(2,1)} %gather_fusion.1) | copy-start | bytes 12582916
  15.6 6.4 %copy-start.2 = (bf16[2,4,16,4,128,128]{5,4,3,1,0,2:T(8,128)(2,1)}, bf16[2,4,16,4,128,128]{5,4,3,1,0,2:T(8,128)(2,1)S(1)}, u32[]{:S(2)}) copy-start(bf16[2,4,16,4,128,128]{5,4,3,1,0,2:T(8,128)(2,1)S(1)} %copy_multiply_fusion) | copy-start | bytes 50331652
  22.0 29.9 %collective-permute-start = (bf16[2,512,512]{2,1,0:T(8,128)(2,1)S(1)}, bf16[2,512,512]{2,1,0:T(8,128)(2,1)S(1)}, u32[]{:S(2)}, u32[]{:S(2)}) collective-permute-start(bf16[2,512,512]{2,1,0:T(8,128)(2,1)S(1)} %get-tuple-element.346), channel_id=1, source_target_pairs={{15,0},{0,1},{1,2},{2,3},{3,4},{4,5},{5,6},{6,7},{7,8},{8,9},{9,10... | collective-permute-start | bytes 3145736 | tf_op jit(solution)/shard_map/while/body/eval_jaxpr/ppermute | solution.py:10
  59.9 26.9 %collective-permute-start = (bf16[2,512,512]{2,1,0:T(8,128)(2,1)S(1)}, bf16[2,512,512]{2,1,0:T(8,128)(2,1)S(1)}, u32[]{:S(2)}, u32[]{:S(2)}) collective-permute-start(bf16[2,512,512]{2,1,0:T(8,128)(2,1)S(1)} %get-tuple-element.346), channel_id=1, source_target_pairs={{15,0},{0,1},{1,2},{2,3},{3,4},{4,5},{5,6},{6,7},{7,8},{8,9},{9,10... | collective-permute-start | bytes 3145736 | tf_op jit(solution)/shard_map/while/body/eval_jaxpr/ppermute | solution.py:10
  94.8 26.0 %collective-permute-start = (bf16[2,512,512]{2,1,0:T(8,128)(2,1)S(1)}, bf16[2,512,512]{2,1,0:T(8,128)(2,1)S(1)}, u32[]{:S(2)}, u32[]{:S(2)}) collective-permute-start(bf16[2,512,512]{2,1,0:T(8,128)(2,1)S(1)} %get-tuple-element.346), channel_id=1, source_target_pairs={{15,0},{0,1},{1,2},{2,3},{3,4},{4,5},{5,6},{6,7},{7,8},{8,9},{9,10... | collective-permute-start | bytes 3145736 | tf_op jit(solution)/shard_map/while/body/eval_jaxpr/ppermute | solution.py:10
  128.9 25.1 %collective-permute-start = (bf16[2,512,512]{2,1,0:T(8,128)(2,1)S(1)}, bf16[2,512,512]{2,1,0:T(8,128)(2,1)S(1)}, u32[]{:S(2)}, u32[]{:S(2)}) collective-permute-start(bf16[2,512,512]{2,1,0:T(8,128)(2,1)S(1)} %get-tuple-element.346), channel_id=1, source_target_pairs={{15,0},{0,1},{1,2},{2,3},{3,4},{4,5},{5,6},{6,7},{7,8},{8,9},{9,10... | collective-permute-start | bytes 3145736 | tf_op jit(solution)/shard_map/while/body/eval_jaxpr/ppermute | solution.py:10
  162.0 24.3 %collective-permute-start = (bf16[2,512,512]{2,1,0:T(8,128)(2,1)S(1)}, bf16[2,512,512]{2,1,0:T(8,128)(2,1)S(1)}, u32[]{:S(2)}, u32[]{:S(2)}) collective-permute-start(bf16[2,512,512]{2,1,0:T(8,128)(2,1)S(1)} %get-tuple-element.346), channel_id=1, source_target_pairs={{15,0},{0,1},{1,2},{2,3},{3,4},{4,5},{5,6},{6,7},{7,8},{8,9},{9,10... | collective-permute-start | bytes 3145736 | tf_op jit(solution)/shard_map/while/body/eval_jaxpr/ppermute | solution.py:10
  194.4 23.4 %collective-permute-start = (bf16[2,512,512]{2,1,0:T(8,128)(2,1)S(1)}, bf16[2,512,512]{2,1,0:T(8,128)(2,1)S(1)}, u32[]{:S(2)}, u32[]{:S(2)}) collective-permute-start(bf16[2,512,512]{2,1,0:T(8,128)(2,1)S(1)} %get-tuple-element.346), channel_id=1, source_target_pairs={{15,0},{0,1},{1,2},{2,3},{3,4},{4,5},{5,6},{6,7},{7,8},{8,9},{9,10... | collective-permute-start | bytes 3145736 | tf_op jit(solution)/shard_map/while/body/eval_jaxpr/ppermute | solution.py:10
  225.8 22.6 %collective-permute-start = (bf16[2,512,512]{2,1,0:T(8,128)(2,1)S(1)}, bf16[2,512,512]{2,1,0:T(8,128)(2,1)S(1)}, u32[]{:S(2)}, u32[]{:S(2)}) collective-permute-start(bf16[2,512,512]{2,1,0:T(8,128)(2,1)S(1)} %get-tuple-element.346), channel_id=1, source_target_pairs={{15,0},{0,1},{1,2},{2,3},{3,4},{4,5},{5,6},{6,7},{7,8},{8,9},{9,10... | collective-permute-start | bytes 3145736 | tf_op jit(solution)/shard_map/while/body/eval_jaxpr/ppermute | solution.py:10
  256.5 21.7 %collective-permute-start = (bf16[2,512,512]{2,1,0:T(8,128)(2,1)S(1)}, bf16[2,512,512]{2,1,0:T(8,128)(2,1)S(1)}, u32[]{:S(2)}, u32[]{:S(2)}) collective-permute-start(bf16[2,512,512]{2,1,0:T(8,128)(2,1)S(1)} %get-tuple-element.346), channel_id=1, source_target_pairs={{15,0},{0,1},{1,2},{2,3},{3,4},{4,5},{5,6},{6,7},{7,8},{8,9},{9,10... | collective-permute-start | bytes 3145736 | tf_op jit(solution)/shard_map/while/body/eval_jaxpr/ppermute | solution.py:10
  286.2 20.8 %collective-permute-start = (bf16[2,512,512]{2,1,0:T(8,128)(2,1)S(1)}, bf16[2,512,512]{2,1,0:T(8,128)(2,1)S(1)}, u32[]{:S(2)}, u32[]{:S(2)}) collective-permute-start(bf16[2,512,512]{2,1,0:T(8,128)(2,1)S(1)} %get-tuple-element.346), channel_id=1, source_target_pairs={{15,0},{0,1},{1,2},{2,3},{3,4},{4,5},{5,6},{6,7},{7,8},{8,9},{9,10... | collective-permute-start | bytes 3145736 | tf_op jit(solution)/shard_map/while/body/eval_jaxpr/ppermute | solution.py:10
  315.1 20.0 %collective-permute-start = (bf16[2,512,512]{2,1,0:T(8,128)(2,1)S(1)}, bf16[2,512,512]{2,1,0:T(8,128)(2,1)S(1)}, u32[]{:S(2)}, u32[]{:S(2)}) collective-permute-start(bf16[2,512,512]{2,1,0:T(8,128)(2,1)S(1)} %get-tuple-element.346), channel_id=1, source_target_pairs={{15,0},{0,1},{1,2},{2,3},{3,4},{4,5},{5,6},{6,7},{7,8},{8,9},{9,10... | collective-permute-start | bytes 3145736 | tf_op jit(solution)/shard_map/while/body/eval_jaxpr/ppermute | solution.py:10
  343.2 19.1 %collective-permute-start = (bf16[2,512,512]{2,1,0:T(8,128)(2,1)S(1)}, bf16[2,512,512]{2,1,0:T(8,128)(2,1)S(1)}, u32[]{:S(2)}, u32[]{:S(2)}) collective-permute-start(bf16[2,512,512]{2,1,0:T(8,128)(2,1)S(1)} %get-tuple-element.346), channel_id=1, source_target_pairs={{15,0},{0,1},{1,2},{2,3},{3,4},{4,5},{5,6},{6,7},{7,8},{8,9},{9,10... | collective-permute-start | bytes 3145736 | tf_op jit(solution)/shard_map/while/body/eval_jaxpr/ppermute | solution.py:10
  370.4 18.3 %collective-permute-start = (bf16[2,512,512]{2,1,0:T(8,128)(2,1)S(1)}, bf16[2,512,512]{2,1,0:T(8,128)(2,1)S(1)}, u32[]{:S(2)}, u32[]{:S(2)}) collective-permute-start(bf16[2,512,512]{2,1,0:T(8,128)(2,1)S(1)} %get-tuple-element.346), channel_id=1, source_target_pairs={{15,0},{0,1},{1,2},{2,3},{3,4},{4,5},{5,6},{6,7},{7,8},{8,9},{9,10... | collective-permute-start | bytes 3145736 | tf_op jit(solution)/shard_map/while/body/eval_jaxpr/ppermute | solution.py:10
  396.7 17.4 %collective-permute-start = (bf16[2,512,512]{2,1,0:T(8,128)(2,1)S(1)}, bf16[2,512,512]{2,1,0:T(8,128)(2,1)S(1)}, u32[]{:S(2)}, u32[]{:S(2)}) collective-permute-start(bf16[2,512,512]{2,1,0:T(8,128)(2,1)S(1)} %get-tuple-element.346), channel_id=1, source_target_pairs={{15,0},{0,1},{1,2},{2,3},{3,4},{4,5},{5,6},{6,7},{7,8},{8,9},{9,10... | collective-permute-start | bytes 3145736 | tf_op jit(solution)/shard_map/while/body/eval_jaxpr/ppermute | solution.py:10
  422.2 17.0 %collective-permute-start = (bf16[2,512,512]{2,1,0:T(8,128)(2,1)S(1)}, bf16[2,512,512]{2,1,0:T(8,128)(2,1)S(1)}, u32[]{:S(2)}, u32[]{:S(2)}) collective-permute-start(bf16[2,512,512]{2,1,0:T(8,128)(2,1)S(1)} %get-tuple-element.346), channel_id=1, source_target_pairs={{15,0},{0,1},{1,2},{2,3},{3,4},{4,5},{5,6},{6,7},{7,8},{8,9},{9,10... | collective-permute-start | bytes 3145736 | tf_op jit(solution)/shard_map/while/body/eval_jaxpr/ppermute | solution.py:10
  447.3 17.0 %collective-permute-start = (bf16[2,512,512]{2,1,0:T(8,128)(2,1)S(1)}, bf16[2,512,512]{2,1,0:T(8,128)(2,1)S(1)}, u32[]{:S(2)}, u32[]{:S(2)}) collective-permute-start(bf16[2,512,512]{2,1,0:T(8,128)(2,1)S(1)} %get-tuple-element.346), channel_id=1, source_target_pairs={{15,0},{0,1},{1,2},{2,3},{3,4},{4,5},{5,6},{6,7},{7,8},{8,9},{9,10... | collective-permute-start | bytes 3145736 | tf_op jit(solution)/shard_map/while/body/eval_jaxpr/ppermute | solution.py:10
  474.3 37.9 %copy-start.1 = (bf16[512,1536]{1,0:T(8,128)(2,1)S(1)}, bf16[512,1536]{1,0:T(8,128)(2,1)}, u32[]{:S(2)}) copy-start(bf16[512,1536]{1,0:T(8,128)(2,1)} %param.19) | copy-start | bytes 4718596
  474.3 37.9 %copy-start.4 = (f32[512]{0:T(512)S(1)}, f32[512]{0:T(512)}, u32[]{:S(2)}) copy-start(f32[512]{0:T(512)} %param.21) | copy-start | bytes 6148
  476.4 33.3 %all-to-all-start = ((bf16[2,512,512]{2,0,1:T(2,128)(2,1)}), bf16[2,512,512]{2,0,1:T(2,128)(2,1)}, u32[]{:S(2)}, u32[]{:S(2)}) async-start(bf16[2,512,512]{2,0,1:T(2,128)(2,1)} %bitcast.70), calls=%async_computation | async-start | bytes 2097152 | tf_op jit(solution)/shard_map/all_to_all | solution.py:67
where the time goes:
time: 595 us; the launch traced here: 593 us
  waiting for transfers between devices  339 us (57%)
  matrix products  130 us (22%)
  local copies, waits for them, and re-layouts  58.6 us (10%)
  other arithmetic  23 us (4%)
  starting transfers between devices  21.4 us (4%)
  blocking collectives  19.4 us (3%)
    ppermute x15, waiting for transfers between devices, shifted(): return lax.ppermute(block, axis, route)  324 us
    dot_general x16, matrix products, partner_sum(): jnp.einsum('snkij,snkjh->snih', tiles_src, picked, preferred_element_type...  80.8 us
    gather x32, local copies, waits for them, and re-layouts, partner_sum(): block_set[col_set]  45.4 us
    dot_general x16, matrix products, gru_cell(): jnp.dot(state.astype(jnp.bfloat16), w_hidden, preferred_element_type=jnp....  28.7 us
    dot_general x16, matrix products, scan_cell(): gx = jnp.dot(graph_row, w_input, preferred_element_type=jnp.float32)  19.5 us
    all_to_all x1, blocking collectives, per_device(): lax.all_to_all(own_seq, 'tm', split_axis=0, concat_axis=1, tiled=True)  19.4 us
    all_to_all x1, starting transfers between devices, per_device(): lax.all_to_all(graph_out, 'tm', split_axis=1, concat_axis=0, tiled=True)  18.2 us
    all_to_all x1, waiting for transfers between devices, per_device(): lax.all_to_all(graph_out, 'tm', split_axis=1, concat_axis=0, tiled=True)  15.1 us
  transfers between devices with their start and end apart: 16, of which 16 were waited for; matrix products, arithmetic and copies ran while one was open for 0% of the time, Pallas kernels for 0%

commit v1 on v0

--- a/solution.py
+++ b/solution.py
@@ -2,6 +2,12 @@
 import jax.numpy as jnp
 from jax import lax
 from jax.sharding import PartitionSpec as P
+
+
+def stacked_exchange(x, mesh_axis, split, join):
+    cells = jnp.split(x, lax.axis_size(mesh_axis), axis=split)
+    received = lax.all_to_all(jnp.stack(cells), mesh_axis, 0, 0)
+    return jnp.concatenate(received, axis=join)
 
 
 def shifted(block, axis, distance):
@@ -64,7 +70,7 @@
     graph_out = jax.nn.relu(propagated).astype(jnp.bfloat16)
     sections = lax.axis_size("tm")
     me_time = lax.axis_index("tm")
-    mine = lax.all_to_all(graph_out, "tm", split_axis=1, concat_axis=0, tiled=True)
+    mine = stacked_exchange(graph_out, "tm", 1, 0)
     share = nodes // sections
     start_rows = lax.dynamic_slice_in_dim(hidden_start, me_time * share, share, 0)
 

time: 595 us -> 596 us (level)
  no operation moved by 1% of the time
where the time goes in v1:
time: 596 us; the launch traced here: 594 us
  waiting for transfers between devices  339 us (57%)
  matrix products  130 us (22%)
  local copies, waits for them, and re-layouts  59.4 us (10%)
  other arithmetic  23.1 us (4%)
  starting transfers between devices  21.4 us (4%)
  blocking collectives  19.4 us (3%)
    ppermute x15, waiting for transfers between devices, shifted(): return lax.ppermute(block, axis, route)  324 us
    dot_general x16, matrix products, partner_sum(): jnp.einsum('snkij,snkjh->snih', tiles_src, picked, preferred_element_type...  80.8 us
    gather x32, local copies, waits for them, and re-layouts, partner_sum(): block_set[col_set]  45.4 us
    dot_general x16, matrix products, gru_cell(): jnp.dot(state.astype(jnp.bfloat16), w_hidden, preferred_element_type=jnp....  28.7 us
    dot_general x16, matrix products, scan_cell(): gx = jnp.dot(graph_row, w_input, preferred_element_type=jnp.float32)  19.5 us
    all_to_all x1, blocking collectives, per_device(): lax.all_to_all(own_seq, 'tm', split_axis=0, concat_axis=1, tiled=True)  19.4 us
    all_to_all x1, starting transfers between devices, stacked_exchange(): received = lax.all_to_all(jnp.stack(cells), mesh_axis, 0, 0)  18.2 us
    all_to_all x1, waiting for transfers between devices, stacked_exchange(): received = lax.all_to_all(jnp.stack(cells), mesh_axis, 0, 0)  15.1 us
  transfers between devices with their start and end apart: 16, of which 16 were waited for; matrix products, arithmetic and copies ran while one was open for 0% of the time, Pallas kernels for 0%

profile of v1, /device:TPU:1, one launch (start us, length us, event | category | flops | bytes accessed | tf_op | source)
XLA Modules:
  0.0 594.1 jit_solution(3788291664134091521)
XLA Ops:
  7.1 8.5 %copy_multiply_fusion = bf16[2,4,16,4,128,128]{5,4,3,1,0,2:T(8,128)(2,1)S(1)} fusion(bf16[2,4,16,4,128,128]{5,4,3,2,1,0:T(8,128)(2,1)} %param.14, bf16[2,4,16,4]{3,1,0,2:T(4,128)(2,1)S(1)} %fusion.36), kind=kLoop, calls=%fused_computation.33 | loop fusion | flops 8388608 | bytes 33555456 | tf_op jit(solution)/shard_map/mul | solution.py:49
  22.0 450.5 %while.29 = (s32[]{:T(128)}, bf16[2,512,512]{2,1,0:T(8,128)(2,1)S(1)}, f32[2,4,128,512]{3,2,1,0:T(8,128)}, s32[]{:T(128)}, bf16[2,4,16,4,128,128]{5,4,3,1,0,2:T(...) while((s32[]{:T(128)}, ...), condition=%wide.region_1.2_spmd, body=%wide.region_0.1_spmd.sunk | while | flops 537395456 | bytes 24118320 | solution.py:68
  24.2 27.7 %collective-permute-done = bf16[2,512,512]{2,1,0:T(8,128)(2,1)S(1)} collective-permute-done((bf16[2,512,512]{2,1,0:T(8,128)(2,1)S(1)}, bf16[2,512,512]{2,1,0:T(8,128)(2,1)S(1)}, u32[]{:S(2)}, u32[]{:S(2)}) %collective-permute-start) | collective-permute-done | bytes 1048608 | tf_op jit(solution)/shard_map/while/body/eval_jaxpr/ppermute | solution.py:16
  54.6 5.2 bitcast_add_fusion.2
  60.1 26.6 %collective-permute-done = bf16[2,512,512]{2,1,0:T(8,128)(2,1)S(1)} collective-permute-done((bf16[2,512,512]{2,1,0:T(8,128)(2,1)S(1)}, bf16[2,512,512]{2,1,0:T(8,128)(2,1)S(1)}, u32[]{:S(2)}, u32[]{:S(2)}) %collective-permute-start) | collective-permute-done | bytes 1048608 | tf_op jit(solution)/shard_map/while/body/eval_jaxpr/ppermute | solution.py:16
  95.0 25.8 %collective-permute-done = bf16[2,512,512]{2,1,0:T(8,128)(2,1)S(1)} collective-permute-done((bf16[2,512,512]{2,1,0:T(8,128)(2,1)S(1)}, bf16[2,512,512]{2,1,0:T(8,128)(2,1)S(1)}, u32[]{:S(2)}, u32[]{:S(2)}) %collective-permute-start) | collective-permute-done | bytes 1048608 | tf_op jit(solution)/shard_map/while/body/eval_jaxpr/ppermute | solution.py:16
  123.5 5.2 bitcast_add_fusion.2
  129.1 24.9 %collective-permute-done = bf16[2,512,512]{2,1,0:T(8,128)(2,1)S(1)} collective-permute-done((bf16[2,512,512]{2,1,0:T(8,128)(2,1)S(1)}, bf16[2,512,512]{2,1,0:T(8,128)(2,1)S(1)}, u32[]{:S(2)}, u32[]{:S(2)}) %collective-permute-start) | collective-permute-done | bytes 1048608 | tf_op jit(solution)/shard_map/while/body/eval_jaxpr/ppermute | solution.py:16
  156.7 5.2 bitcast_add_fusion.2
  162.2 24.1 %collective-permute-done = bf16[2,512,512]{2,1,0:T(8,128)(2,1)S(1)} collective-permute-done((bf16[2,512,512]{2,1,0:T(8,128)(2,1)S(1)}, bf16[2,512,512]{2,1,0:T(8,128)(2,1)S(1)}, u32[]{:S(2)}, u32[]{:S(2)}) %collective-permute-start) | collective-permute-done | bytes 1048608 | tf_op jit(solution)/shard_map/while/body/eval_jaxpr/ppermute | solution.py:16
  189.1 5.2 bitcast_add_fusion.2
  194.6 23.2 %collective-permute-done = bf16[2,512,512]{2,1,0:T(8,128)(2,1)S(1)} collective-permute-done((bf16[2,512,512]{2,1,0:T(8,128)(2,1)S(1)}, bf16[2,512,512]{2,1,0:T(8,128)(2,1)S(1)}, u32[]{:S(2)}, u32[]{:S(2)}) %collective-permute-start) | collective-permute-done | bytes 1048608 | tf_op jit(solution)/shard_map/while/body/eval_jaxpr/ppermute | solution.py:16
  220.5 5.2 bitcast_add_fusion.2
  226.1 22.4 %collective-permute-done = bf16[2,512,512]{2,1,0:T(8,128)(2,1)S(1)} collective-permute-done((bf16[2,512,512]{2,1,0:T(8,128)(2,1)S(1)}, bf16[2,512,512]{2,1,0:T(8,128)(2,1)S(1)}, u32[]{:S(2)}, u32[]{:S(2)}) %collective-permute-start) | collective-permute-done | bytes 1048608 | tf_op jit(solution)/shard_map/while/body/eval_jaxpr/ppermute | solution.py:16
  251.2 5.2 bitcast_add_fusion.2
  256.7 21.5 %collective-permute-done = bf16[2,512,512]{2,1,0:T(8,128)(2,1)S(1)} collective-permute-done((bf16[2,512,512]{2,1,0:T(8,128)(2,1)S(1)}, bf16[2,512,512]{2,1,0:T(8,128)(2,1)S(1)}, u32[]{:S(2)}, u32[]{:S(2)}) %collective-permute-start) | collective-permute-done | bytes 1048608 | tf_op jit(solution)/shard_map/while/body/eval_jaxpr/ppermute | solution.py:16
  286.4 20.6 %collective-permute-done = bf16[2,512,512]{2,1,0:T(8,128)(2,1)S(1)} collective-permute-done((bf16[2,512,512]{2,1,0:T(8,128)(2,1)S(1)}, bf16[2,512,512]{2,1,0:T(8,128)(2,1)S(1)}, u32[]{:S(2)}, u32[]{:S(2)}) %collective-permute-start) | collective-permute-done | bytes 1048608 | tf_op jit(solution)/shard_map/while/body/eval_jaxpr/ppermute | solution.py:16
  309.8 5.2 bitcast_add_fusion.2
  315.4 19.8 %collective-permute-done = bf16[2,512,512]{2,1,0:T(8,128)(2,1)S(1)} collective-permute-done((bf16[2,512,512]{2,1,0:T(8,128)(2,1)S(1)}, bf16[2,512,512]{2,1,0:T(8,128)(2,1)S(1)}, u32[]{:S(2)}, u32[]{:S(2)}) %collective-permute-start) | collective-permute-done | bytes 1048608 | tf_op jit(solution)/shard_map/while/body/eval_jaxpr/ppermute | solution.py:16
  337.9 5.2 bitcast_add_fusion.2
  343.4 18.9 %collective-permute-done = bf16[2,512,512]{2,1,0:T(8,128)(2,1)S(1)} collective-permute-done((bf16[2,512,512]{2,1,0:T(8,128)(2,1)S(1)}, bf16[2,512,512]{2,1,0:T(8,128)(2,1)S(1)}, u32[]{:S(2)}, u32[]{:S(2)}) %collective-permute-start) | collective-permute-done | bytes 1048608 | tf_op jit(solution)/shard_map/while/body/eval_jaxpr/ppermute | solution.py:16
  365.1 5.2 bitcast_add_fusion.2
  370.6 18.1 %collective-permute-done = bf16[2,512,512]{2,1,0:T(8,128)(2,1)S(1)} collective-permute-done((bf16[2,512,512]{2,1,0:T(8,128)(2,1)S(1)}, bf16[2,512,512]{2,1,0:T(8,128)(2,1)S(1)}, u32[]{:S(2)}, u32[]{:S(2)}) %collective-permute-start) | collective-permute-done | bytes 1048608 | tf_op jit(solution)/shard_map/while/body/eval_jaxpr/ppermute | solution.py:16
  397.0 17.2 %collective-permute-done = bf16[2,512,512]{2,1,0:T(8,128)(2,1)S(1)} collective-permute-done((bf16[2,512,512]{2,1,0:T(8,128)(2,1)S(1)}, bf16[2,512,512]{2,1,0:T(8,128)(2,1)S(1)}, u32[]{:S(2)}, u32[]{:S(2)}) %collective-permute-start) | collective-permute-done | bytes 1048608 | tf_op jit(solution)/shard_map/while/body/eval_jaxpr/ppermute | solution.py:16
  422.4 16.8 %collective-permute-done = bf16[2,512,512]{2,1,0:T(8,128)(2,1)S(1)} collective-permute-done((bf16[2,512,512]{2,1,0:T(8,128)(2,1)S(1)}, bf16[2,512,512]{2,1,0:T(8,128)(2,1)S(1)}, u32[]{:S(2)}, u32[]{:S(2)}) %collective-permute-start) | collective-permute-done | bytes 1048608 | tf_op jit(solution)/shard_map/while/body/eval_jaxpr/ppermute | solution.py:16
  442.0 5.2 bitcast_add_fusion.2
  447.5 16.8 %collective-permute-done = bf16[2,512,512]{2,1,0:T(8,128)(2,1)S(1)} collective-permute-done((bf16[2,512,512]{2,1,0:T(8,128)(2,1)S(1)}, bf16[2,512,512]{2,1,0:T(8,128)(2,1)S(1)}, u32[]{:S(2)}, u32[]{:S(2)}) %collective-permute-start) | collective-permute-done | bytes 1048608 | tf_op jit(solution)/shard_map/while/body/eval_jaxpr/ppermute | solution.py:16
  467.1 5.2 bitcast_add_fusion.2
  479.8 18.2 %all-to-all-start = ((bf16[8,2,64,512]{3,2,1,0:T(8,128)(2,1)}), bf16[8,2,64,512]{3,2,1,0:T(8,128)(2,1)}, u32[]{:S(2)}, u32[]{:S(2)}) async-start(bf16[8,2,64,512]{3,2,1,0:T(8,128)(2,1)} %fusion.27), calls=%async_computation | async-start | bytes 2097152 | tf_op jit(solution)/shard_map/all_to_all | solution.py:9
  498.0 15.1 %all-to-all-done = bf16[8,2,64,512]{3,2,1,0:T(8,128)(2,1)} async-done(((bf16[8,2,64,512]{3,2,1,0:T(8,128)(2,1)}), bf16[8,2,64,512]{3,2,1,0:T(8,128)(2,1)}, u32[]{:S(2)}, u32[]{:S(2)}) %all-to-all-start) | async-done | bytes 1048608 | tf_op jit(solution)/shard_map/all_to_all | solution.py:9
  513.0 60.7 %while.30 = (s32[]{:T(128)}, f32[64,512]{1,0:T(8,128)S(1)}, bf16[16,64,512]{2,1,0:T(8,128)(2,1)}, bf16[16,64,512]{2,1,0:T(8,128)(2,1)}, bf16[512,1536]{1,0:T(8,1...) while((s32[]{:T(128)}, f32[64,512]{1,0:T(8,128)S(1)}, ...), condition=%wide.region_3.4_spmd, body=%wide.region_2.3_spmd.sunk | while | flops 201883648 | bytes 5246037 | solution.py:82
  573.7 19.4 %all_to_all.23 = bf16[16,64,512]{2,1,0:T(8,128)(2,1)S(1)} all-to-all(bf16[16,64,512]{2,1,0:T(8,128)(2,1)} %get-tuple-element.198), channel_id=1, replica_groups=mesh['tm'=8,'dom'=16] {'tm'}, dimensions={0} | all-to-all | bytes 2097152 | tf_op jit(solution)/shard_map/all_to_all | solution.py:83
  (158 shorter events, 150.1 us)
Async XLA Ops:
  0.0 498.0 %copy-start = (f32[512,512]{1,0:T(8,128)S(1)}, f32[512,512]{1,0:T(8,128)}, u32[]{:S(2)}) copy-start(f32[512,512]{1,0:T(8,128)} %param.17) | copy-start | bytes 3145732
  7.1 8.5 %copy-start.3 = (bf16[32,128,512]{2,1,0:T(8,128)(2,1)S(1)}, bf16[32,128,512]{2,1,0:T(8,128)(2,1)}, u32[]{:S(2)}) copy-start(bf16[32,128,512]{2,1,0:T(8,128)(2,1)} %gather_fusion.1) | copy-start | bytes 12582916
  15.6 6.4 %copy-start.2 = (bf16[2,4,16,4,128,128]{5,4,3,1,0,2:T(8,128)(2,1)}, bf16[2,4,16,4,128,128]{5,4,3,1,0,2:T(8,128)(2,1)S(1)}, u32[]{:S(2)}) copy-start(bf16[2,4,16,4,128,128]{5,4,3,1,0,2:T(8,128)(2,1)S(1)} %copy_multiply_fusion) | copy-start | bytes 50331652
  22.0 29.9 %collective-permute-start = (bf16[2,512,512]{2,1,0:T(8,128)(2,1)S(1)}, bf16[2,512,512]{2,1,0:T(8,128)(2,1)S(1)}, u32[]{:S(2)}, u32[]{:S(2)}) collective-permute-start(bf16[2,512,512]{2,1,0:T(8,128)(2,1)S(1)} %get-tuple-element.334), channel_id=1, source_target_pairs={{15,0},{0,1},{1,2},{2,3},{3,4},{4,5},{5,6},{6,7},{7,8},{8,9},{9,10... | collective-permute-start | bytes 3145736 | tf_op jit(solution)/shard_map/while/body/eval_jaxpr/ppermute | solution.py:16
  59.9 26.9 %collective-permute-start = (bf16[2,512,512]{2,1,0:T(8,128)(2,1)S(1)}, bf16[2,512,512]{2,1,0:T(8,128)(2,1)S(1)}, u32[]{:S(2)}, u32[]{:S(2)}) collective-permute-start(bf16[2,512,512]{2,1,0:T(8,128)(2,1)S(1)} %get-tuple-element.334), channel_id=1, source_target_pairs={{15,0},{0,1},{1,2},{2,3},{3,4},{4,5},{5,6},{6,7},{7,8},{8,9},{9,10... | collective-permute-start | bytes 3145736 | tf_op jit(solution)/shard_map/while/body/eval_jaxpr/ppermute | solution.py:16
  94.8 26.0 %collective-permute-start = (bf16[2,512,512]{2,1,0:T(8,128)(2,1)S(1)}, bf16[2,512,512]{2,1,0:T(8,128)(2,1)S(1)}, u32[]{:S(2)}, u32[]{:S(2)}) collective-permute-start(bf16[2,512,512]{2,1,0:T(8,128)(2,1)S(1)} %get-tuple-element.334), channel_id=1, source_target_pairs={{15,0},{0,1},{1,2},{2,3},{3,4},{4,5},{5,6},{6,7},{7,8},{8,9},{9,10... | collective-permute-start | bytes 3145736 | tf_op jit(solution)/shard_map/while/body/eval_jaxpr/ppermute | solution.py:16
  128.9 25.1 %collective-permute-start = (bf16[2,512,512]{2,1,0:T(8,128)(2,1)S(1)}, bf16[2,512,512]{2,1,0:T(8,128)(2,1)S(1)}, u32[]{:S(2)}, u32[]{:S(2)}) collective-permute-start(bf16[2,512,512]{2,1,0:T(8,128)(2,1)S(1)} %get-tuple-element.334), channel_id=1, source_target_pairs={{15,0},{0,1},{1,2},{2,3},{3,4},{4,5},{5,6},{6,7},{7,8},{8,9},{9,10... | collective-permute-start | bytes 3145736 | tf_op jit(solution)/shard_map/while/body/eval_jaxpr/ppermute | solution.py:16
  162.0 24.3 %collective-permute-start = (bf16[2,512,512]{2,1,0:T(8,128)(2,1)S(1)}, bf16[2,512,512]{2,1,0:T(8,128)(2,1)S(1)}, u32[]{:S(2)}, u32[]{:S(2)}) collective-permute-start(bf16[2,512,512]{2,1,0:T(8,128)(2,1)S(1)} %get-tuple-element.334), channel_id=1, source_target_pairs={{15,0},{0,1},{1,2},{2,3},{3,4},{4,5},{5,6},{6,7},{7,8},{8,9},{9,10... | collective-permute-start | bytes 3145736 | tf_op jit(solution)/shard_map/while/body/eval_jaxpr/ppermute | solution.py:16
  194.4 23.4 %collective-permute-start = (bf16[2,512,512]{2,1,0:T(8,128)(2,1)S(1)}, bf16[2,512,512]{2,1,0:T(8,128)(2,1)S(1)}, u32[]{:S(2)}, u32[]{:S(2)}) collective-permute-start(bf16[2,512,512]{2,1,0:T(8,128)(2,1)S(1)} %get-tuple-element.334), channel_id=1, source_target_pairs={{15,0},{0,1},{1,2},{2,3},{3,4},{4,5},{5,6},{6,7},{7,8},{8,9},{9,10... | collective-permute-start | bytes 3145736 | tf_op jit(solution)/shard_map/while/body/eval_jaxpr/ppermute | solution.py:16
  225.8 22.6 %collective-permute-start = (bf16[2,512,512]{2,1,0:T(8,128)(2,1)S(1)}, bf16[2,512,512]{2,1,0:T(8,128)(2,1)S(1)}, u32[]{:S(2)}, u32[]{:S(2)}) collective-permute-start(bf16[2,512,512]{2,1,0:T(8,128)(2,1)S(1)} %get-tuple-element.334), channel_id=1, source_target_pairs={{15,0},{0,1},{1,2},{2,3},{3,4},{4,5},{5,6},{6,7},{7,8},{8,9},{9,10... | collective-permute-start | bytes 3145736 | tf_op jit(solution)/shard_map/while/body/eval_jaxpr/ppermute | solution.py:16
  256.5 21.7 %collective-permute-start = (bf16[2,512,512]{2,1,0:T(8,128)(2,1)S(1)}, bf16[2,512,512]{2,1,0:T(8,128)(2,1)S(1)}, u32[]{:S(2)}, u32[]{:S(2)}) collective-permute-start(bf16[2,512,512]{2,1,0:T(8,128)(2,1)S(1)} %get-tuple-element.334), channel_id=1, source_target_pairs={{15,0},{0,1},{1,2},{2,3},{3,4},{4,5},{5,6},{6,7},{7,8},{8,9},{9,10... | collective-permute-start | bytes 3145736 | tf_op jit(solution)/shard_map/while/body/eval_jaxpr/ppermute | solution.py:16
  286.2 20.8 %collective-permute-start = (bf16[2,512,512]{2,1,0:T(8,128)(2,1)S(1)}, bf16[2,512,512]{2,1,0:T(8,128)(2,1)S(1)}, u32[]{:S(2)}, u32[]{:S(2)}) collective-permute-start(bf16[2,512,512]{2,1,0:T(8,128)(2,1)S(1)} %get-tuple-element.334), channel_id=1, source_target_pairs={{15,0},{0,1},{1,2},{2,3},{3,4},{4,5},{5,6},{6,7},{7,8},{8,9},{9,10... | collective-permute-start | bytes 3145736 | tf_op jit(solution)/shard_map/while/body/eval_jaxpr/ppermute | solution.py:16
  315.1 20.0 %collective-permute-start = (bf16[2,512,512]{2,1,0:T(8,128)(2,1)S(1)}, bf16[2,512,512]{2,1,0:T(8,128)(2,1)S(1)}, u32[]{:S(2)}, u32[]{:S(2)}) collective-permute-start(bf16[2,512,512]{2,1,0:T(8,128)(2,1)S(1)} %get-tuple-element.334), channel_id=1, source_target_pairs={{15,0},{0,1},{1,2},{2,3},{3,4},{4,5},{5,6},{6,7},{7,8},{8,9},{9,10... | collective-permute-start | bytes 3145736 | tf_op jit(solution)/shard_map/while/body/eval_jaxpr/ppermute | solution.py:16
  343.2 19.1 %collective-permute-start = (bf16[2,512,512]{2,1,0:T(8,128)(2,1)S(1)}, bf16[2,512,512]{2,1,0:T(8,128)(2,1)S(1)}, u32[]{:S(2)}, u32[]{:S(2)}) collective-permute-start(bf16[2,512,512]{2,1,0:T(8,128)(2,1)S(1)} %get-tuple-element.334), channel_id=1, source_target_pairs={{15,0},{0,1},{1,2},{2,3},{3,4},{4,5},{5,6},{6,7},{7,8},{8,9},{9,10... | collective-permute-start | bytes 3145736 | tf_op jit(solution)/shard_map/while/body/eval_jaxpr/ppermute | solution.py:16
  370.4 18.3 %collective-permute-start = (bf16[2,512,512]{2,1,0:T(8,128)(2,1)S(1)}, bf16[2,512,512]{2,1,0:T(8,128)(2,1)S(1)}, u32[]{:S(2)}, u32[]{:S(2)}) collective-permute-start(bf16[2,512,512]{2,1,0:T(8,128)(2,1)S(1)} %get-tuple-element.334), channel_id=1, source_target_pairs={{15,0},{0,1},{1,2},{2,3},{3,4},{4,5},{5,6},{6,7},{7,8},{8,9},{9,10... | collective-permute-start | bytes 3145736 | tf_op jit(solution)/shard_map/while/body/eval_jaxpr/ppermute | solution.py:16
  396.7 17.4 %collective-permute-start = (bf16[2,512,512]{2,1,0:T(8,128)(2,1)S(1)}, bf16[2,512,512]{2,1,0:T(8,128)(2,1)S(1)}, u32[]{:S(2)}, u32[]{:S(2)}) collective-permute-start(bf16[2,512,512]{2,1,0:T(8,128)(2,1)S(1)} %get-tuple-element.334), channel_id=1, source_target_pairs={{15,0},{0,1},{1,2},{2,3},{3,4},{4,5},{5,6},{6,7},{7,8},{8,9},{9,10... | collective-permute-start | bytes 3145736 | tf_op jit(solution)/shard_map/while/body/eval_jaxpr/ppermute | solution.py:16
  422.2 17.0 %collective-permute-start = (bf16[2,512,512]{2,1,0:T(8,128)(2,1)S(1)}, bf16[2,512,512]{2,1,0:T(8,128)(2,1)S(1)}, u32[]{:S(2)}, u32[]{:S(2)}) collective-permute-start(bf16[2,512,512]{2,1,0:T(8,128)(2,1)S(1)} %get-tuple-element.334), channel_id=1, source_target_pairs={{15,0},{0,1},{1,2},{2,3},{3,4},{4,5},{5,6},{6,7},{7,8},{8,9},{9,10... | collective-permute-start | bytes 3145736 | tf_op jit(solution)/shard_map/while/body/eval_jaxpr/ppermute | solution.py:16
  447.3 17.0 %collective-permute-start = (bf16[2,512,512]{2,1,0:T(8,128)(2,1)S(1)}, bf16[2,512,512]{2,1,0:T(8,128)(2,1)S(1)}, u32[]{:S(2)}, u32[]{:S(2)}) collective-permute-start(bf16[2,512,512]{2,1,0:T(8,128)(2,1)S(1)} %get-tuple-element.334), channel_id=1, source_target_pairs={{15,0},{0,1},{1,2},{2,3},{3,4},{4,5},{5,6},{6,7},{7,8},{8,9},{9,10... | collective-permute-start | bytes 3145736 | tf_op jit(solution)/shard_map/while/body/eval_jaxpr/ppermute | solution.py:16
  472.4 40.6 %copy-start.1 = (bf16[512,1536]{1,0:T(8,128)(2,1)S(1)}, bf16[512,1536]{1,0:T(8,128)(2,1)}, u32[]{:S(2)}) copy-start(bf16[512,1536]{1,0:T(8,128)(2,1)} %param.19) | copy-start | bytes 4718596
  472.4 40.6 %copy-start.4 = (f32[512]{0:T(512)S(1)}, f32[512]{0:T(512)}, u32[]{:S(2)}) copy-start(f32[512]{0:T(512)} %param.21) | copy-start | bytes 6148
  479.8 33.3 %all-to-all-start = ((bf16[8,2,64,512]{3,2,1,0:T(8,128)(2,1)}), bf16[8,2,64,512]{3,2,1,0:T(8,128)(2,1)}, u32[]{:S(2)}, u32[]{:S(2)}) async-start(bf16[8,2,64,512]{3,2,1,0:T(8,128)(2,1)} %fusion.27), calls=%async_computation | async-start | bytes 2097152 | tf_op jit(solution)/shard_map/all_to_all | solution.py:9
